TPU v7x, 32 devices: a whole 2x2x4 slice. The times are simulated.
32 devices in a mesh: outer: 4 (over y, x), inner: 8 (over z, core).
Axes of the slice: x: 2, y: 2, z: 4, core: 2. Of those that a mesh axis runs over, the one named last changes fastest.
Arguments:
- queries: bfloat16 [4096, 2048], P(('outer', 'inner')), may hold values from -6 to 6
- key_rows: bfloat16 [4096, 2048], P(('outer', 'inner')), may hold values from -6 to 6
- value_rows: bfloat16 [4096, 2048], P(('outer', 'inner')), may hold values from -6 to 6
- beta_logit: bfloat16 [4096, 16], P(('outer', 'inner')), may hold values from -8 to 2, as said below
- log_gate: bfloat16 [4096, 16], P(('outer', 'inner')), may hold values from -1 to 0, as said below
- out_grad: bfloat16 [4096, 2048], P(('outer', 'inner')), may hold values from -6 to 6
- block_states: float32 [4, 16, 128, 128], P('outer', 'inner'), may hold values from -4 to 4
Outputs:
- query_gradient: bfloat16 [4096, 2048], P(('outer', 'inner'))
- grad_keys: bfloat16 [4096, 2048], P(('outer', 'inner'))
- grad_values: bfloat16 [4096, 2048], P(('outer', 'inner'))
- grad_beta: bfloat16 [4096, 16], P(('outer', 'inner'))
- grad_gate: bfloat16 [4096, 16], P(('outer', 'inner'))
Inputs may be any that keep to these rules, and one draw needn't show every extreme that they name: `beta_logit`: within each head the logits lie within 1 of a level drawn for each head. `log_gate`: negative in every entry.
All inputs are finite; a program needn't handle non-finite values.
Results may differ from a plain program's by a relative error of at most 0.002.
Values may be sent and summed in bfloat16 or wider, within the bound.
A program may use at most 128 MiB of HBM per device.

v0:
```python
import jax
import jax.numpy as jnp
from jax import lax
from jax.sharding import PartitionSpec as P

DK = 128
DV = 128
GROUP = 128
precise = lax.Precision.HIGHEST


def unit_rows(matrix):
    return matrix * lax.rsqrt(jnp.sum(matrix * matrix, axis=-1, keepdims=True) + 1e-06)


def group_step(carried, inputs):
    state_now, transition, grad_sum = carried
    query_part, key_part, value_part, strength, gate_part, cotangent_part = inputs
    group_len = query_part.shape[1]
    key_width = key_part.shape[2]
    row_index = jnp.arange(group_len)[:, None]
    col_index = jnp.arange(group_len)[None, :]
    inclusive = row_index >= col_index
    strictly_lower = row_index > col_index
    cumulative = jnp.cumsum(gate_part, axis=1)
    gaps = cumulative[:, :, None] - cumulative[:, None, :]
    decay_mat = jnp.where(inclusive, jnp.exp(jnp.where(inclusive, gaps, 0.0)), 0.0)
    key_gram = jnp.einsum("hid,hjd->hij", key_part, key_part, precision=precise)
    lower_mat = strength[:, :, None] * jnp.where(strictly_lower, decay_mat, 0.0) * key_gram
    unit_lower = lower_mat + jnp.eye(group_len, dtype=jnp.float32)
    growth = jnp.exp(cumulative)
    right_side = jnp.concatenate(
        [(strength * growth)[:, :, None] * key_part, strength[:, :, None] * value_part], axis=2
    )
    solution_matrix = lax.linalg.triangular_solve(
        unit_lower, right_side, left_side=True, lower=True, unit_diagonal=True
    )
    write_keys = solution_matrix[:, :, :key_width]
    write_values = solution_matrix[:, :, key_width:]
    new_values = write_values - jnp.einsum("hcd,hde->hce", write_keys, state_now, precision=precise)
    scores = jnp.einsum("hid,hjd->hij", query_part, key_part, precision=precise) * decay_mat
    grown_queries = query_part * growth[:, :, None]
    output = jnp.einsum("hcd,hde->hce", grown_queries, state_now, precision=precise)
    output = output + jnp.einsum("hij,hje->hie", scores, new_values, precision=precise)
    tail_decay = jnp.exp(cumulative[:, -1:] - cumulative)
    tail_keys = key_part * tail_decay[:, :, None]
    last_growth = growth[:, -1][:, None, None]
    state_next = last_growth * state_now + jnp.einsum(
        "hcd,hce->hde", tail_keys, new_values, precision=precise
    )
    detached = lax.stop_gradient
    state_queries = detached(
        grown_queries - jnp.einsum("hij,hjd->hid", scores, write_keys, precision=precise)
    )
    projected = jnp.einsum("hcd,hce->hde", state_queries, cotangent_part, precision=precise)
    grad_sum = grad_sum + jnp.einsum("hji,hje->hie", transition, projected, precision=precise)
    step_trans = detached(
        last_growth * jnp.eye(key_width, dtype=jnp.float32)
        - jnp.einsum("hcd,hce->hde", tail_keys, write_keys, precision=precise)
    )
    transition = jnp.einsum("hij,hjk->hik", step_trans, transition, precision=precise)
    return ((state_next, transition, grad_sum), output)


def block_forward(queries, keys_in, values, logits, gates, start_state, cotangent, group_size):
    head_count, length, key_width = queries.shape
    group_count = length // group_size

    def to_groups(array_in):
        shaped = array_in.reshape((head_count, group_count, group_size) + array_in.shape[2:])
        return jnp.moveaxis(shaped, 1, 0)

    inputs = (
        to_groups(unit_rows(queries)),
        to_groups(unit_rows(keys_in)),
        to_groups(values),
        to_groups(jax.nn.sigmoid(logits)),
        to_groups(gates),
        to_groups(cotangent),
    )
    identity = jnp.broadcast_to(
        jnp.eye(key_width, dtype=jnp.float32), (head_count, key_width, key_width)
    )
    grad_zero = jnp.zeros(start_state.shape, jnp.float32)
    (final_state, transition, grad_sum), outputs = lax.scan(
        group_step, (start_state, identity, grad_zero), inputs
    )
    outputs = jnp.moveaxis(outputs, 0, 1).reshape(head_count, length, -1)
    return ((outputs, final_state), (transition, grad_sum))


def matmul_heads(left_mat, right_mat):
    return jnp.einsum("hij,hjk->hik", left_mat, right_mat, precision=precise)


def head_split(array_in, width):
    return array_in.astype(jnp.float32).reshape(array_in.shape[0], -1, width).transpose(1, 0, 2)


def merge_heads(array_in):
    return array_in.transpose(1, 0, 2).reshape(array_in.shape[1], -1).astype(jnp.bfloat16)


def prepare(queries, key_rows, value_rows, out_grad, beta_logit, log_gate):
    return (
        head_split(queries, DK),
        head_split(key_rows, DK),
        head_split(value_rows, DV),
        beta_logit.astype(jnp.float32).T,
        log_gate.astype(jnp.float32).T,
        head_split(out_grad, DV),
    )


def block_pullback(pieces, start_state):
    query_in, key_in, value_in, logit_in, gate_in, cotangent = pieces

    def forward(query_arg, key_arg, value_arg, logit_arg, gate_arg, state_arg):
        return block_forward(
            query_arg, key_arg, value_arg, logit_arg, gate_arg, state_arg, cotangent, GROUP
        )

    unused_out, pull_back, side = jax.vjp(
        forward, query_in, key_in, value_in, logit_in, gate_in, start_state, has_aux=True
    )
    turned = jnp.swapaxes(side[0], 1, 2)

    def finish(incoming):
        gradients = pull_back((cotangent, incoming))
        return gradients[:5]

    return (turned, side[1], finish)


def fold_later(matrices, state_grads, position):
    total_blocks = matrices.shape[0]

    def advance(turn_index, running):
        block_index = total_blocks - 1 - turn_index
        updated = matmul_heads(matrices[block_index], running) + state_grads[block_index]
        return jnp.where(block_index > position, updated, running)

    return lax.fori_loop(0, total_blocks, advance, jnp.zeros_like(state_grads[0]))


def shards(queries, key_rows, value_rows, beta_logit, log_gate, out_grad, block_states):
    arrived = (
        lax.all_to_all(queries, "inner", split_axis=1, concat_axis=0, tiled=True),
        lax.all_to_all(key_rows, "inner", split_axis=1, concat_axis=0, tiled=True),
        lax.all_to_all(value_rows, "inner", split_axis=1, concat_axis=0, tiled=True),
        lax.all_to_all(out_grad, "inner", split_axis=1, concat_axis=0, tiled=True),
        lax.all_to_all(beta_logit, "inner", split_axis=1, concat_axis=0, tiled=True),
        lax.all_to_all(log_gate, "inner", split_axis=1, concat_axis=0, tiled=True),
    )
    pieces = prepare(arrived[0], arrived[1], arrived[2], arrived[3], arrived[4], arrived[5])
    start_state = block_states[0]
    turned, grad_start, finish = block_pullback(pieces, start_state)
    gathered = (
        lax.all_gather(turned[None], "outer", axis=0, tiled=True),
        lax.all_gather(grad_start[None], "outer", axis=0, tiled=True),
    )
    incoming = fold_later(gathered[0], gathered[1], lax.axis_index("outer"))
    gradients = finish(incoming)
    result = (
        lax.all_to_all(merge_heads(gradients[0]), "inner", split_axis=0, concat_axis=1, tiled=True),
        lax.all_to_all(merge_heads(gradients[1]), "inner", split_axis=0, concat_axis=1, tiled=True),
        lax.all_to_all(merge_heads(gradients[2]), "inner", split_axis=0, concat_axis=1, tiled=True),
        lax.all_to_all(
            gradients[3].T.astype(jnp.bfloat16), "inner", split_axis=0, concat_axis=1, tiled=True
        ),
        lax.all_to_all(
            gradients[4].T.astype(jnp.bfloat16), "inner", split_axis=0, concat_axis=1, tiled=True
        ),
    )
    return (result[0], result[1], result[2], result[3], result[4])


def solution(mesh):
    return jax.shard_map(
        shards,
        mesh=mesh,
        in_specs=(
            P(("outer", "inner"), None),
            P(("outer", "inner"), None),
            P(("outer", "inner"), None),
            P(("outer", "inner"), None),
            P(("outer", "inner"), None),
            P(("outer", "inner"), None),
            P("outer", "inner", None, None),
        ),
        out_specs=(
            P(("outer", "inner"), None),
            P(("outer", "inner"), None),
            P(("outer", "inner"), None),
            P(("outer", "inner"), None),
            P(("outer", "inner"), None),
        ),
        check_vma=False,
    )
```

profile of v0, /device:TPU:0, one launch (start us, length us, event | category | flops | bytes accessed | tf_op | source)
XLA Modules:
  0.0 874.6 jit_solution(8195031747380546615)
XLA Ops:
  0.6 11.9 %all_to_all.164 = bf16[128,8,2]{0,2,1:T(2,128)(2,1)S(1)} all-to-all(bf16[128,8,2]{0,2,1:T(2,128)(2,1)} %bitcast.638), channel_id=1, replica_groups=mesh['outer'=4,'inner'=8] {'inner'}, dimensions={1} | all-to-all | bytes 8192 | tf_op jit(solution)/shard_map/all_to_all | solution.py:152
  12.6 3.3 all-to-all-start
  18.0 3.3 all-to-all-done
  21.3 3.6 all-to-all-start.1
  26.0 14.3 %all-to-all-done.1 = bf16[128,8,256]{0,2,1:T(8,128)(2,1)S(1)} async-done(((bf16[128,8,256]{0,2,1:T(8,128)(2,1)}), bf16[128,8,256]{0,2,1:T(8,128)(2,1)S(1)}, u32[]{:S(2)}, u32[]{:S(2)}) %all-to-all-start.1) | async-done | bytes 524320 | tf_op jit(solution)/shard_map/all_to_all | solution.py:149
  40.2 3.5 all-to-all-start.4
  47.6 11.4 %all-to-all-done.4 = bf16[128,8,256]{0,2,1:T(8,128)(2,1)S(1)} async-done(((bf16[128,8,256]{0,2,1:T(8,128)(2,1)}), bf16[128,8,256]{0,2,1:T(8,128)(2,1)S(1)}, u32[]{:S(2)}, u32[]{:S(2)}) %all-to-all-start.4) | async-done | bytes 524320 | tf_op jit(solution)/shard_map/all_to_all | solution.py:148
  59.0 4.1 all-to-all-start.3
  64.4 14.2 %all-to-all-done.3 = bf16[128,8,256]{0,2,1:T(8,128)(2,1)} async-done(((bf16[128,8,256]{0,2,1:T(8,128)(2,1)}), bf16[128,8,256]{0,2,1:T(8,128)(2,1)}, u32[]{:S(2)}, u32[]{:S(2)}) %all-to-all-start.3) | async-done | bytes 524320 | tf_op jit(solution)/shard_map/all_to_all | solution.py:150
  78.5 4.3 all-to-all-start.5
  91.0 2.5 copy.350
  96.3 2.4 reshape.533
  98.6 2.6 copy.347
  106.2 2.4 reshape.534
  108.6 2.6 copy.353
  111.2 2.3 copy.359
  113.6 269.3 %while.108 = (s32[]{:T(128)}, f32[2,128,128]{2,1,0:T(8,128)S(1)}, f32[2,128,128]{2,1,0:T(8,128)S(1)}, f32[2,128,128]{1,2,0:T(8,128)S(1)}, f32[8,2,128,128]{3,2,1...) while((s32[]{:T(128)}, f32[2,128,128]{2,1,0:T(8,128)S(1)}, ...), condition=%wide.region_4.5_spmd.clone.clone, body=%wide.region_2.4_spmd.clone.clone.sunk | while | flops 555172992 | bytes 8843675 | solution.py:85
  118.0 19.7 %custom-call.48 = f32[2,1,128,128]{2,3,1,0:T(8,128)S(1)} custom-call(f32[2,1,128,128]{3,2,1,0:T(8,128)S(1)} %get-tuple-element.3072), custom_call_target="InvertDiagBlocksLowerTriangular" | custom-call | tf_op jit(solution)/shard_map/jvp()/while/body/eval_jaxpr/triangular_solve | solution.py:35
  151.6 19.7 %custom-call.48 = f32[2,1,128,128]{2,3,1,0:T(8,128)S(1)} custom-call(f32[2,1,128,128]{3,2,1,0:T(8,128)S(1)} %get-tuple-element.3072), custom_call_target="InvertDiagBlocksLowerTriangular" | custom-call | tf_op jit(solution)/shard_map/jvp()/while/body/eval_jaxpr/triangular_solve | solution.py:35
  185.3 19.7 %custom-call.48 = f32[2,1,128,128]{2,3,1,0:T(8,128)S(1)} custom-call(f32[2,1,128,128]{3,2,1,0:T(8,128)S(1)} %get-tuple-element.3072), custom_call_target="InvertDiagBlocksLowerTriangular" | custom-call | tf_op jit(solution)/shard_map/jvp()/while/body/eval_jaxpr/triangular_solve | solution.py:35
  219.0 19.7 %custom-call.48 = f32[2,1,128,128]{2,3,1,0:T(8,128)S(1)} custom-call(f32[2,1,128,128]{3,2,1,0:T(8,128)S(1)} %get-tuple-element.3072), custom_call_target="InvertDiagBlocksLowerTriangular" | custom-call | tf_op jit(solution)/shard_map/jvp()/while/body/eval_jaxpr/triangular_solve | solution.py:35
  252.6 19.7 %custom-call.48 = f32[2,1,128,128]{2,3,1,0:T(8,128)S(1)} custom-call(f32[2,1,128,128]{3,2,1,0:T(8,128)S(1)} %get-tuple-element.3072), custom_call_target="InvertDiagBlocksLowerTriangular" | custom-call | tf_op jit(solution)/shard_map/jvp()/while/body/eval_jaxpr/triangular_solve | solution.py:35
  286.3 19.7 %custom-call.48 = f32[2,1,128,128]{2,3,1,0:T(8,128)S(1)} custom-call(f32[2,1,128,128]{3,2,1,0:T(8,128)S(1)} %get-tuple-element.3072), custom_call_target="InvertDiagBlocksLowerTriangular" | custom-call | tf_op jit(solution)/shard_map/jvp()/while/body/eval_jaxpr/triangular_solve | solution.py:35
  319.9 19.7 %custom-call.48 = f32[2,1,128,128]{2,3,1,0:T(8,128)S(1)} custom-call(f32[2,1,128,128]{3,2,1,0:T(8,128)S(1)} %get-tuple-element.3072), custom_call_target="InvertDiagBlocksLowerTriangular" | custom-call | tf_op jit(solution)/shard_map/jvp()/while/body/eval_jaxpr/triangular_solve | solution.py:35
  353.6 19.7 %custom-call.48 = f32[2,1,128,128]{2,3,1,0:T(8,128)S(1)} custom-call(f32[2,1,128,128]{3,2,1,0:T(8,128)S(1)} %get-tuple-element.3072), custom_call_target="InvertDiagBlocksLowerTriangular" | custom-call | tf_op jit(solution)/shard_map/jvp()/while/body/eval_jaxpr/triangular_solve | solution.py:35
  383.0 11.4 %all-gather = f32[8,128,128]{2,1,0:T(8,128)} all-gather(f32[2,128,128]{2,1,0:T(8,128)S(1)} %bitcast.630), channel_id=2, replica_groups=mesh['outer'=4,'inner'=8] {'outer'}, dimensions={0}, use_global_device_ids=true | all-gather | bytes 655360 | tf_op jit(solution)/shard_map/all_gather | solution.py:159
  394.5 10.2 %all-gather.1 = f32[8,128,128]{2,1,0:T(8,128)} all-gather(f32[2,128,128]{2,1,0:T(8,128)S(1)} %copy.361), channel_id=3, replica_groups=mesh['outer'=4,'inner'=8] {'outer'}, dimensions={0}, use_global_device_ids=true | all-gather | bytes 655360 | tf_op jit(solution)/shard_map/all_gather | solution.py:160
  404.7 5.2 while.107
  412.0 380.4 %while.106 = (s32[]{:T(128)}, f32[2,128,128]{2,1,0:T(8,128)S(1)}, f32[8,2,128,128]{3,2,0,1:T(8,128)}, f32[8,2,128,128]{3,2,0,1:T(8,128)}, bf16[8,2,128,128]{3,2,...) while((s32[]{:T(128)}, f32[2,128,128]{2,1,0:T(8,128)S(1)}, ...), condition=%wide.region_18.19_spmd.clone.clone, body=%wide.region_7.18_spmd.clone.clone.sunk | while | flops 857327744 | bytes 11667445 | solution.py:85
  416.9 19.7 %custom-call.47 = f32[2,1,128,128]{2,3,1,0:T(8,128)S(1)} custom-call(f32[2,1,128,128]{3,2,1,0:T(8,128)S(1)} %add_bitcast_fusion.4), custom_call_target="InvertDiagBlocksLowerTriangular" | custom-call | tf_op jit(solution)/shard_map/transpose(jvp())/while/body/eval_jaxpr/triangular_solve | solution.py:35
  464.4 19.7 %custom-call.47 = f32[2,1,128,128]{2,3,1,0:T(8,128)S(1)} custom-call(f32[2,1,128,128]{3,2,1,0:T(8,128)S(1)} %add_bitcast_fusion.4), custom_call_target="InvertDiagBlocksLowerTriangular" | custom-call | tf_op jit(solution)/shard_map/transpose(jvp())/while/body/eval_jaxpr/triangular_solve | solution.py:35
  512.0 19.7 %custom-call.47 = f32[2,1,128,128]{2,3,1,0:T(8,128)S(1)} custom-call(f32[2,1,128,128]{3,2,1,0:T(8,128)S(1)} %add_bitcast_fusion.4), custom_call_target="InvertDiagBlocksLowerTriangular" | custom-call | tf_op jit(solution)/shard_map/transpose(jvp())/while/body/eval_jaxpr/triangular_solve | solution.py:35
  559.6 19.7 %custom-call.47 = f32[2,1,128,128]{2,3,1,0:T(8,128)S(1)} custom-call(f32[2,1,128,128]{3,2,1,0:T(8,128)S(1)} %add_bitcast_fusion.4), custom_call_target="InvertDiagBlocksLowerTriangular" | custom-call | tf_op jit(solution)/shard_map/transpose(jvp())/while/body/eval_jaxpr/triangular_solve | solution.py:35
  607.1 19.7 %custom-call.47 = f32[2,1,128,128]{2,3,1,0:T(8,128)S(1)} custom-call(f32[2,1,128,128]{3,2,1,0:T(8,128)S(1)} %add_bitcast_fusion.4), custom_call_target="InvertDiagBlocksLowerTriangular" | custom-call | tf_op jit(solution)/shard_map/transpose(jvp())/while/body/eval_jaxpr/triangular_solve | solution.py:35
  654.7 19.7 %custom-call.47 = f32[2,1,128,128]{2,3,1,0:T(8,128)S(1)} custom-call(f32[2,1,128,128]{3,2,1,0:T(8,128)S(1)} %add_bitcast_fusion.4), custom_call_target="InvertDiagBlocksLowerTriangular" | custom-call | tf_op jit(solution)/shard_map/transpose(jvp())/while/body/eval_jaxpr/triangular_solve | solution.py:35
  702.2 19.7 %custom-call.47 = f32[2,1,128,128]{2,3,1,0:T(8,128)S(1)} custom-call(f32[2,1,128,128]{3,2,1,0:T(8,128)S(1)} %add_bitcast_fusion.4), custom_call_target="InvertDiagBlocksLowerTriangular" | custom-call | tf_op jit(solution)/shard_map/transpose(jvp())/while/body/eval_jaxpr/triangular_solve | solution.py:35
  749.8 19.7 %custom-call.47 = f32[2,1,128,128]{2,3,1,0:T(8,128)S(1)} custom-call(f32[2,1,128,128]{3,2,1,0:T(8,128)S(1)} %add_bitcast_fusion.4), custom_call_target="InvertDiagBlocksLowerTriangular" | custom-call | tf_op jit(solution)/shard_map/transpose(jvp())/while/body/eval_jaxpr/triangular_solve | solution.py:35
  792.4 2.6 copy.376
  797.0 4.8 all-to-all-start.9
  801.8 5.5 all-to-all-done.9
  807.3 3.3 all-to-all-start.10
  813.0 3.0 all-to-all-done.10
  816.0 3.5 all-to-all-start.7
  822.5 12.3 %all-to-all-done.7 = bf16[8,128,256]{1,2,0:T(8,128)(2,1)S(1)} async-done(((bf16[8,128,256]{1,2,0:T(8,128)(2,1)}), bf16[8,128,256]{1,2,0:T(8,128)(2,1)S(1)}, u32[]{:S(2)}, u32[]{:S(2)}) %all-to-all-start.7) | async-done | bytes 524320 | tf_op jit(solution)/shard_map/all_to_all | solution.py:166
  834.8 3.5 all-to-all-start.6
  839.5 14.1 %all-to-all-done.6 = bf16[8,128,256]{1,2,0:T(8,128)(2,1)S(1)} async-done(((bf16[8,128,256]{1,2,0:T(8,128)(2,1)}), bf16[8,128,256]{1,2,0:T(8,128)(2,1)S(1)}, u32[]{:S(2)}, u32[]{:S(2)}) %all-to-all-start.6) | async-done | bytes 524320 | tf_op jit(solution)/shard_map/all_to_all | solution.py:165
  853.6 3.5 all-to-all-start.8
  859.1 13.3 %all-to-all-done.8 = bf16[8,128,256]{1,2,0:T(8,128)(2,1)S(1)} async-done(((bf16[8,128,256]{1,2,0:T(8,128)(2,1)}), bf16[8,128,256]{1,2,0:T(8,128)(2,1)S(1)}, u32[]{:S(2)}, u32[]{:S(2)}) %all-to-all-start.8) | async-done | bytes 524320 | tf_op jit(solution)/shard_map/all_to_all | solution.py:167
  (613 shorter events, 376.5 us)
Async XLA Ops:
  0.6 24.3 %copy-start.5 = (bf16[128,2048]{1,0:T(8,128)(2,1)S(1)}, bf16[128,2048]{1,0:T(8,128)(2,1)}, u32[]{:S(2)}) copy-start(bf16[128,2048]{1,0:T(8,128)(2,1)} %param.13) | copy-start | bytes 1572868
  12.6 8.7 all-to-all-start
  15.9 28.0 %copy-start.6 = (bf16[128,2048]{1,0:T(8,128)(2,1)S(1)}, bf16[128,2048]{1,0:T(8,128)(2,1)}, u32[]{:S(2)}) copy-start(bf16[128,2048]{1,0:T(8,128)(2,1)} %param.15) | copy-start | bytes 1572868
  21.3 23.6 %copy-start.7 = (bf16[128,2048]{1,0:T(8,128)(2,1)S(1)}, bf16[128,2048]{1,0:T(8,128)(2,1)}, u32[]{:S(2)}) copy-start(bf16[128,2048]{1,0:T(8,128)(2,1)} %param.18) | copy-start | bytes 1572868
  21.3 18.9 %all-to-all-start.1 = ((bf16[128,8,256]{0,2,1:T(8,128)(2,1)}), bf16[128,8,256]{0,2,1:T(8,128)(2,1)S(1)}, u32[]{:S(2)}, u32[]{:S(2)}) async-start(bf16[128,8,256]{0,2,1:T(8,128)(2,1)} %bitcast.6), calls=%async_computation.1 | async-start | bytes 1048576 | tf_op jit(solution)/shard_map/all_to_all | solution.py:149
  40.2 18.8 %all-to-all-start.4 = ((bf16[128,8,256]{0,2,1:T(8,128)(2,1)}), bf16[128,8,256]{0,2,1:T(8,128)(2,1)S(1)}, u32[]{:S(2)}, u32[]{:S(2)}) async-start(bf16[128,8,256]{0,2,1:T(8,128)(2,1)} %bitcast.20), calls=%async_computation.4 | async-start | bytes 1048576 | tf_op jit(solution)/shard_map/all_to_all | solution.py:148
  59.0 19.5 %all-to-all-start.3 = ((bf16[128,8,256]{0,2,1:T(8,128)(2,1)}), bf16[128,8,256]{0,2,1:T(8,128)(2,1)}, u32[]{:S(2)}, u32[]{:S(2)}) async-start(bf16[128,8,256]{0,2,1:T(8,128)(2,1)} %bitcast.15), calls=%async_computation.3 | async-start | bytes 1048576 | tf_op jit(solution)/shard_map/all_to_all | solution.py:150
  64.1 14.4 %copy-start.1 = (f32[1024,2,128]{0,2,1:T(8,128)}, f32[1024,2,128]{0,2,1:T(8,128)S(1)}, u32[]{:S(2)}) copy-start(f32[1024,2,128]{0,2,1:T(8,128)S(1)} %reshape.528) | copy-start | bytes 3145732
  78.5 25.0 %all-to-all-start.5 = ((bf16[128,8,256]{0,2,1:T(8,128)(2,1)}), bf16[128,8,256]{0,2,1:T(8,128)(2,1)}, u32[]{:S(2)}, u32[]{:S(2)}) async-start(bf16[128,8,256]{0,2,1:T(8,128)(2,1)} %bitcast.622), calls=%async_computation.5 | async-start | bytes 1048576 | tf_op jit(solution)/shard_map/all_to_all | solution.py:151
  85.2 1.5 copy-start.3
  108.6 5.0 copy-start
  792.4 2.7 copy-start.2
  797.0 10.3 %all-to-all-start.9 = ((bf16[8,128,2]{1,2,0:T(2,128)(2,1)}), bf16[8,128,2]{1,2,0:T(2,128)(2,1)S(1)}, u32[]{:S(2)}, u32[]{:S(2)}) async-start(bf16[8,128,2]{1,2,0:T(2,128)(2,1)} %fusion.167), calls=%async_computation.9 | async-start | bytes 8192 | tf_op jit(solution)/shard_map/all_to_all | solution.py:168
  807.3 8.7 all-to-all-start.10
  816.0 18.8 %all-to-all-start.7 = ((bf16[8,128,256]{1,2,0:T(8,128)(2,1)}), bf16[8,128,256]{1,2,0:T(8,128)(2,1)S(1)}, u32[]{:S(2)}, u32[]{:S(2)}) async-start(bf16[8,128,256]{1,2,0:T(8,128)(2,1)} %copy.378), calls=%async_computation.7 | async-start | bytes 1048576 | tf_op jit(solution)/shard_map/all_to_all | solution.py:166
  821.5 16.8 %copy-start.4 = (bf16[8,2,128,128]{3,2,0,1:T(8,128)(2,1)S(1)}, bf16[8,2,128,128]{3,2,0,1:T(8,128)(2,1)}, u32[]{:S(2)}) copy-start(bf16[8,2,128,128]{3,2,0,1:T(8,128)(2,1)} %get-tuple-element.1507) | copy-start | bytes 1572868
  834.8 18.8 %all-to-all-start.6 = ((bf16[8,128,256]{1,2,0:T(8,128)(2,1)}), bf16[8,128,256]{1,2,0:T(8,128)(2,1)S(1)}, u32[]{:S(2)}, u32[]{:S(2)}) async-start(bf16[8,128,256]{1,2,0:T(8,128)(2,1)} %copy.374), calls=%async_computation.6 | async-start | bytes 1048576 | tf_op jit(solution)/shard_map/all_to_all | solution.py:165
  853.6 18.8 %all-to-all-start.8 = ((bf16[8,128,256]{1,2,0:T(8,128)(2,1)}), bf16[8,128,256]{1,2,0:T(8,128)(2,1)S(1)}, u32[]{:S(2)}, u32[]{:S(2)}) async-start(bf16[8,128,256]{1,2,0:T(8,128)(2,1)} %copy.381), calls=%async_computation.8 | async-start | bytes 1048576 | tf_op jit(solution)/shard_map/all_to_all | solution.py:167
where the time goes:
time: 880 us; the launch traced here: 875 us
  other arithmetic  406 us (46%)
  matrix products  225 us (26%)
  waiting for transfers between devices  91.2 us (10%)
  local copies, waits for them, and re-layouts  77.8 us (9%)
  starting transfers between devices  37.5 us (4%)
  blocking collectives  33.5 us (4%)
    another operation x80, other arithmetic, group_step(): lax.linalg.triangular_solve(unit_lower, right_side, left_side=True, lower...  332 us
    dot_general x24, matrix products, group_step(): jnp.einsum('hid,hjd->hij', query_part, key_part, precision=precise)  38.8 us
    dynamic_update_slice x48, other arithmetic, block_forward(): lax.scan(group_step, (start_state, identity, grad_zero), inputs)  38.2 us
    dot_general x24, matrix products, group_step(): key_gram = jnp.einsum('hid,hjd->hij', key_part, key_part, precision=precise)  28.3 us
    dot_general x24, matrix products, group_step(): jnp.einsum('hcd,hde->hce', write_keys, state_now, precision=precise)  28.1 us
    dot_general x24, matrix products, group_step(): jnp.einsum('hcd,hce->hde', tail_keys, new_values, precision=precise)  25.2 us
    dot_general x16, matrix products, group_step(): jnp.einsum('hij,hje->hie', scores, new_values, precision=precise)  23.9 us
    dot_general x16, matrix products, group_step(): jnp.einsum('hcd,hde->hce', grown_queries, state_now, precision=precise)  21.9 us
  transfers between devices with their start and end apart: 10, of which 9 were waited for; matrix products, arithmetic and copies ran while one was open for 4% of the time, Pallas kernels for 0%

commit v1 on v0

--- a/solution.py
+++ b/solution.py
@@ -1,3 +1,4 @@
+import functools
 import jax
 import jax.numpy as jnp
 from jax import lax
@@ -7,6 +8,30 @@
 DV = 128
 GROUP = 128
 precise = lax.Precision.HIGHEST
+
+
+def spans_name(local_values, link_axis):
+    val2 = lax.axis_size(link_axis)
+    reply = lax.axis_index(link_axis)
+    w2, spare = (val2, reply)
+    p_next = local_values.shape[1] // w2
+    outcome_arr = list(local_values.shape)
+    outcome_arr[1] = p_next
+    arr_now = outcome_arr[0]
+    outcome_arr[0] = arr_now * w2
+    ready = jnp.zeros(outcome_arr, local_values.dtype)
+    for pp in range(w2):
+        before = lax.dynamic_slice_in_dim(local_values, (spare ^ pp) * p_next, p_next, axis=1)
+        if pp:
+            xs_all = []
+            for q in range(w2):
+                xs_all.append((q, q ^ pp))
+            before = lax.ppermute(before, link_axis, xs_all)
+        ready = lax.dynamic_update_slice_in_dim(ready, before, (spare ^ pp) * arr_now, axis=0)
+    return ready
+
+
+halves_part = functools.partial(spans_name, link_axis="inner")
 
 
 def unit_rows(matrix):
@@ -146,7 +171,7 @@
 def shards(queries, key_rows, value_rows, beta_logit, log_gate, out_grad, block_states):
     arrived = (
         lax.all_to_all(queries, "inner", split_axis=1, concat_axis=0, tiled=True),
-        lax.all_to_all(key_rows, "inner", split_axis=1, concat_axis=0, tiled=True),
+        halves_part(key_rows),
         lax.all_to_all(value_rows, "inner", split_axis=1, concat_axis=0, tiled=True),
         lax.all_to_all(out_grad, "inner", split_axis=1, concat_axis=0, tiled=True),
         lax.all_to_all(beta_logit, "inner", split_axis=1, concat_axis=0, tiled=True),

time: 880 us -> 1070 us (1.22)
  other arithmetic: 406 us -> 488 us
  local copies, waits for them, and re-layouts: 77.8 us -> 141 us
  matrix products: 225 us -> 274 us
  blocking collectives: 33.5 us -> 21.6 us
  starting transfers between devices: 37.5 us -> 48.8 us
  waiting for transfers between devices: 91.2 us -> 80.2 us
    another operation x24, other arithmetic: 13.3 us -> 33.1 us  [group_step(): cumulative = jnp.cumsum(gate_part, axis=1)]
    dynamic_update_slice x48, other arithmetic: 38.2 us -> 57.9 us  [block_forward(): lax.scan(group_step, (start_state, identity, grad_zero), inputs)]
    another operation x80, other arithmetic: 332 us -> 349 us  [group_step(): lax.linalg.triangular_solve(unit_lower, right_side, left_side=True, lower...]
    while x12 -> x188, local copies, waits for them, and re-layouts: 0.13 us -> 16.7 us
    another operation x24, matrix products: 15.2 us -> 28.1 us  [group_step(): lax.linalg.triangular_solve(unit_lower, right_side, left_side=True, lower...]
    all_to_all x1 -> x0, blocking collectives: 11.9 us -> none  [shards(): lax.all_to_all(beta_logit, 'inner', split_axis=1, concat_axis=0, tiled=True)]
    dot_general x8, matrix products: 2.19 us -> 13.7 us  [group_step(): jnp.einsum('hji,hje->hie', transition, projected, precision=precise)]
    all_to_all x1, waiting for transfers between devices: 14.3 us -> 3.03 us  [shards(): lax.all_to_all(beta_logit, 'inner', split_axis=1, concat_axis=0, tiled=True)]
  transfers between devices with their start and end apart: 10 -> 17, of which waited for: 9 -> 9; matrix products, arithmetic and copies ran while one was open for 4% -> 3% of each run, Pallas kernels for 0% -> 0%
where the time goes in v1:
time: 1070 us; the launch traced here: 1060 us
  other arithmetic  488 us (46%)
  matrix products  274 us (26%)
  local copies, waits for them, and re-layouts  141 us (13%)
  waiting for transfers between devices  80.2 us (7%)
  starting transfers between devices  48.8 us (5%)
  blocking collectives  21.6 us (2%)
    another operation x80, other arithmetic, group_step(): lax.linalg.triangular_solve(unit_lower, right_side, left_side=True, lower...  349 us
    dynamic_update_slice x48, other arithmetic, block_forward(): lax.scan(group_step, (start_state, identity, grad_zero), inputs)  57.9 us
    dot_general x24, matrix products, group_step(): jnp.einsum('hid,hjd->hij', query_part, key_part, precision=precise)  39.3 us
    dot_general x24, matrix products, group_step(): jnp.einsum('hcd,hce->hde', tail_keys, new_values, precision=precise)  34 us
    another operation x24, other arithmetic, group_step(): cumulative = jnp.cumsum(gate_part, axis=1)  33.1 us
    dot_general x16, matrix products, group_step(): jnp.einsum('hij,hje->hie', scores, new_values, precision=precise)  28.7 us
    dot_general x24, matrix products, group_step(): key_gram = jnp.einsum('hid,hjd->hij', key_part, key_part, precision=precise)  28.2 us
    dot_general x24, matrix products, group_step(): jnp.einsum('hcd,hde->hce', write_keys, state_now, precision=precise)  28.2 us
  transfers between devices with their start and end apart: 17, of which 9 were waited for; matrix products, arithmetic and copies ran while one was open for 3% of the time, Pallas kernels for 0%

profile of v1, /device:TPU:0, one launch (start us, length us, event | category | flops | bytes accessed | tf_op | source)
XLA Modules:
  0.0 1057.4 jit_solution(9382843355796998001)
XLA Ops:
  2.6 2.7 collective-permute-start.1
  5.7 2.8 collective-permute-start.3
  8.7 4.9 all-to-all-start.1
  16.1 3.0 all-to-all-done.1
  19.1 3.3 all-to-all-start
  24.0 3.8 all-to-all-done
  27.8 3.5 all-to-all-start.3
  35.6 3.8 collective-permute-start.5
  39.6 10.3 all-to-all-done.3
  49.9 4.2 all-to-all-start.2
  55.6 13.8 %all-to-all-done.2 = bf16[128,8,256]{0,2,1:T(8,128)(2,1)} async-done(((bf16[128,8,256]{0,2,1:T(8,128)(2,1)}), bf16[128,8,256]{0,2,1:T(8,128)(2,1)}, u32[]{:S(2)}, u32[]{:S(2)}) %all-to-all-start.2) | async-done | bytes 524320 | tf_op jit(solution)/shard_map/all_to_all | solution.py:175
  69.4 4.3 all-to-all-start.4
  95.7 2.6 copy.381
  102.5 346.6 %while.108 = (s32[]{:T(128)}, f32[2,128,128]{2,1,0:T(8,128)S(1)}, f32[2,128,128]{2,1,0:T(8,128)}, f32[2,128,128]{1,2,0:T(8,128)}, f32[8,2,128,128]{3,2,1,0:T(8,1...) while((s32[]{:T(128)}, f32[2,128,128]{2,1,0:T(8,128)S(1)}, ...), condition=%wide.region_4.5_spmd.clone.clone, body=%wide.region_2.4_spmd.clone.clone.sunk | while | flops 555172992 | bytes 8860807 | solution.py:110
  109.4 21.1 %custom-call.48 = f32[2,1,128,128]{2,3,1,0:T(8,128)} custom-call(f32[2,1,128,128]{3,2,1,0:T(8,128)} %get-tuple-element.3080), custom_call_target="InvertDiagBlocksLowerTriangular" | custom-call | tf_op jit(solution)/shard_map/jvp()/while/body/eval_jaxpr/triangular_solve | solution.py:60
  151.9 21.1 %custom-call.48 = f32[2,1,128,128]{2,3,1,0:T(8,128)} custom-call(f32[2,1,128,128]{3,2,1,0:T(8,128)} %get-tuple-element.3080), custom_call_target="InvertDiagBlocksLowerTriangular" | custom-call | tf_op jit(solution)/shard_map/jvp()/while/body/eval_jaxpr/triangular_solve | solution.py:60
  195.4 21.1 %custom-call.48 = f32[2,1,128,128]{2,3,1,0:T(8,128)} custom-call(f32[2,1,128,128]{3,2,1,0:T(8,128)} %get-tuple-element.3080), custom_call_target="InvertDiagBlocksLowerTriangular" | custom-call | tf_op jit(solution)/shard_map/jvp()/while/body/eval_jaxpr/triangular_solve | solution.py:60
  238.8 21.1 %custom-call.48 = f32[2,1,128,128]{2,3,1,0:T(8,128)} custom-call(f32[2,1,128,128]{3,2,1,0:T(8,128)} %get-tuple-element.3080), custom_call_target="InvertDiagBlocksLowerTriangular" | custom-call | tf_op jit(solution)/shard_map/jvp()/while/body/eval_jaxpr/triangular_solve | solution.py:60
  282.3 21.1 %custom-call.48 = f32[2,1,128,128]{2,3,1,0:T(8,128)} custom-call(f32[2,1,128,128]{3,2,1,0:T(8,128)} %get-tuple-element.3080), custom_call_target="InvertDiagBlocksLowerTriangular" | custom-call | tf_op jit(solution)/shard_map/jvp()/while/body/eval_jaxpr/triangular_solve | solution.py:60
  325.7 21.1 %custom-call.48 = f32[2,1,128,128]{2,3,1,0:T(8,128)} custom-call(f32[2,1,128,128]{3,2,1,0:T(8,128)} %get-tuple-element.3080), custom_call_target="InvertDiagBlocksLowerTriangular" | custom-call | tf_op jit(solution)/shard_map/jvp()/while/body/eval_jaxpr/triangular_solve | solution.py:60
  369.2 21.1 %custom-call.48 = f32[2,1,128,128]{2,3,1,0:T(8,128)} custom-call(f32[2,1,128,128]{3,2,1,0:T(8,128)} %get-tuple-element.3080), custom_call_target="InvertDiagBlocksLowerTriangular" | custom-call | tf_op jit(solution)/shard_map/jvp()/while/body/eval_jaxpr/triangular_solve | solution.py:60
  412.6 21.1 %custom-call.48 = f32[2,1,128,128]{2,3,1,0:T(8,128)} custom-call(f32[2,1,128,128]{3,2,1,0:T(8,128)} %get-tuple-element.3080), custom_call_target="InvertDiagBlocksLowerTriangular" | custom-call | tf_op jit(solution)/shard_map/jvp()/while/body/eval_jaxpr/triangular_solve | solution.py:60
  450.1 11.4 %all-gather = f32[8,128,128]{2,1,0:T(8,128)} all-gather(f32[2,128,128]{2,1,0:T(8,128)S(1)} %bitcast.636), channel_id=2, replica_groups=mesh['outer'=4,'inner'=8] {'outer'}, dimensions={0}, use_global_device_ids=true | all-gather | bytes 655360 | tf_op jit(solution)/shard_map/all_gather | solution.py:184
  462.4 10.2 all-gather.1
  472.6 5.2 while.107
  480.6 496.8 %while.106 = (s32[]{:T(128)}, f32[2,128,128]{2,1,0:T(8,128)S(1)}, f32[8,2,128,128]{3,2,0,1:T(8,128)}, f32[8,2,128,128]{3,2,0,1:T(8,128)}, bf16[8,2,128,128]{3,2,...) while((s32[]{:T(128)}, f32[2,128,128]{2,1,0:T(8,128)S(1)}, ...), condition=%wide.region_18.19_spmd.clone.clone, body=%wide.region_7.18_spmd.clone.clone.sunk | while | flops 857327744 | bytes 11688065 | solution.py:110
  485.5 19.7 %custom-call.47 = f32[2,1,128,128]{2,3,1,0:T(8,128)S(1)} custom-call(f32[2,1,128,128]{3,2,1,0:T(8,128)S(1)} %add_bitcast_fusion.4), custom_call_target="InvertDiagBlocksLowerTriangular" | custom-call | tf_op jit(solution)/shard_map/transpose(jvp())/while/body/eval_jaxpr/triangular_solve | solution.py:60
  516.6 2.6 fusion.276
  547.6 19.7 %custom-call.47 = f32[2,1,128,128]{2,3,1,0:T(8,128)S(1)} custom-call(f32[2,1,128,128]{3,2,1,0:T(8,128)S(1)} %add_bitcast_fusion.4), custom_call_target="InvertDiagBlocksLowerTriangular" | custom-call | tf_op jit(solution)/shard_map/transpose(jvp())/while/body/eval_jaxpr/triangular_solve | solution.py:60
  578.6 2.6 fusion.276
  609.6 19.7 %custom-call.47 = f32[2,1,128,128]{2,3,1,0:T(8,128)S(1)} custom-call(f32[2,1,128,128]{3,2,1,0:T(8,128)S(1)} %add_bitcast_fusion.4), custom_call_target="InvertDiagBlocksLowerTriangular" | custom-call | tf_op jit(solution)/shard_map/transpose(jvp())/while/body/eval_jaxpr/triangular_solve | solution.py:60
  671.8 19.7 %custom-call.47 = f32[2,1,128,128]{2,3,1,0:T(8,128)S(1)} custom-call(f32[2,1,128,128]{3,2,1,0:T(8,128)S(1)} %add_bitcast_fusion.4), custom_call_target="InvertDiagBlocksLowerTriangular" | custom-call | tf_op jit(solution)/shard_map/transpose(jvp())/while/body/eval_jaxpr/triangular_solve | solution.py:60
  734.0 19.7 %custom-call.47 = f32[2,1,128,128]{2,3,1,0:T(8,128)S(1)} custom-call(f32[2,1,128,128]{3,2,1,0:T(8,128)S(1)} %add_bitcast_fusion.4), custom_call_target="InvertDiagBlocksLowerTriangular" | custom-call | tf_op jit(solution)/shard_map/transpose(jvp())/while/body/eval_jaxpr/triangular_solve | solution.py:60
  765.0 2.6 fusion.276
  796.0 19.7 %custom-call.47 = f32[2,1,128,128]{2,3,1,0:T(8,128)S(1)} custom-call(f32[2,1,128,128]{3,2,1,0:T(8,128)S(1)} %add_bitcast_fusion.4), custom_call_target="InvertDiagBlocksLowerTriangular" | custom-call | tf_op jit(solution)/shard_map/transpose(jvp())/while/body/eval_jaxpr/triangular_solve | solution.py:60
  827.1 2.6 fusion.276
  858.1 19.7 %custom-call.47 = f32[2,1,128,128]{2,3,1,0:T(8,128)S(1)} custom-call(f32[2,1,128,128]{3,2,1,0:T(8,128)S(1)} %add_bitcast_fusion.4), custom_call_target="InvertDiagBlocksLowerTriangular" | custom-call | tf_op jit(solution)/shard_map/transpose(jvp())/while/body/eval_jaxpr/triangular_solve | solution.py:60
  920.3 19.7 %custom-call.47 = f32[2,1,128,128]{2,3,1,0:T(8,128)S(1)} custom-call(f32[2,1,128,128]{3,2,1,0:T(8,128)S(1)} %add_bitcast_fusion.4), custom_call_target="InvertDiagBlocksLowerTriangular" | custom-call | tf_op jit(solution)/shard_map/transpose(jvp())/while/body/eval_jaxpr/triangular_solve | solution.py:60
  979.8 4.8 all-to-all-start.8
  984.6 5.5 all-to-all-done.8
  990.1 3.3 all-to-all-start.9
  994.6 4.3 all-to-all-done.9
  998.8 3.5 all-to-all-start.6
  1005.4 12.2 %all-to-all-done.6 = bf16[8,128,256]{1,2,0:T(8,128)(2,1)S(1)} async-done(((bf16[8,128,256]{1,2,0:T(8,128)(2,1)}), bf16[8,128,256]{1,2,0:T(8,128)(2,1)S(1)}, u32[]{:S(2)}, u32[]{:S(2)}) %all-to-all-start.6) | async-done | bytes 524320 | tf_op jit(solution)/shard_map/all_to_all | solution.py:191
  1017.6 3.5 all-to-all-start.5
  1022.4 14.0 %all-to-all-done.5 = bf16[8,128,256]{1,2,0:T(8,128)(2,1)S(1)} async-done(((bf16[8,128,256]{1,2,0:T(8,128)(2,1)}), bf16[8,128,256]{1,2,0:T(8,128)(2,1)S(1)}, u32[]{:S(2)}, u32[]{:S(2)}) %all-to-all-start.5) | async-done | bytes 524320 | tf_op jit(solution)/shard_map/all_to_all | solution.py:190
  1036.4 3.5 all-to-all-start.7
  1041.9 13.3 %all-to-all-done.7 = bf16[8,128,256]{1,2,0:T(8,128)(2,1)S(1)} async-done(((bf16[8,128,256]{1,2,0:T(8,128)(2,1)}), bf16[8,128,256]{1,2,0:T(8,128)(2,1)S(1)}, u32[]{:S(2)}, u32[]{:S(2)}) %all-to-all-start.7) | async-done | bytes 524320 | tf_op jit(solution)/shard_map/all_to_all | solution.py:192
  (842 shorter events, 564.5 us)
Async XLA Ops:
  0.6 22.4 %copy-start.4 = (bf16[128,2048]{1,0:T(8,128)(2,1)S(1)}, bf16[128,2048]{1,0:T(8,128)(2,1)}, u32[]{:S(2)}) copy-start(bf16[128,2048]{1,0:T(8,128)(2,1)} %param.13) | copy-start | bytes 1572868
  2.0 33.7 %collective-permute-start = (bf16[128,256]{0,1:T(8,128)(2,1)S(1)}, bf16[128,256]{0,1:T(8,128)(2,1)S(1)}, u32[]{:S(2)}, u32[]{:S(2)}) collective-permute-start(bf16[128,256]{0,1:T(8,128)(2,1)S(1)} %copy.440), channel_id=1, source_target_pairs={{0,1},{1,0},{2,3},{3,2},{4,5},{5,4},{6,7},{7,6},{8,9},{9,8},{10,11... | collective-permute-start | bytes 196616 | tf_op jit(solution)/shard_map/ppermute | solution.py:29
  2.6 36.8 %collective-permute-start.1 = (bf16[128,256]{0,1:T(8,128)(2,1)S(1)}, bf16[128,256]{0,1:T(8,128)(2,1)S(1)}, u32[]{:S(2)}, u32[]{:S(2)}) collective-permute-start(bf16[128,256]{0,1:T(8,128)(2,1)S(1)} %copy.441), channel_id=1, source_target_pairs={{0,2},{1,3},{2,0},{3,1},{4,6},{5,7},{6,4},{7,5},{8,10},{9,11},{10,... | collective-permute-start | bytes 196616 | tf_op jit(solution)/shard_map/ppermute | solution.py:29
  5.4 27.0 %copy-start.5 = (bf16[128,2048]{1,0:T(8,128)(2,1)S(1)}, bf16[128,2048]{1,0:T(8,128)(2,1)}, u32[]{:S(2)}) copy-start(bf16[128,2048]{1,0:T(8,128)(2,1)} %param.15) | copy-start | bytes 1572868
  5.4 34.1 %collective-permute-start.2 = (bf16[128,256]{0,1:T(8,128)(2,1)S(1)}, bf16[128,256]{0,1:T(8,128)(2,1)S(1)}, u32[]{:S(2)}, u32[]{:S(2)}) collective-permute-start(bf16[128,256]{0,1:T(8,128)(2,1)S(1)} %copy.442), channel_id=1, source_target_pairs={{0,3},{1,2},{2,1},{3,0},{4,7},{5,6},{6,5},{7,4},{8,11},{9,10},{10,... | collective-permute-start | bytes 196616 | tf_op jit(solution)/shard_map/ppermute | solution.py:29
  5.7 33.9 %collective-permute-start.3 = (bf16[128,256]{0,1:T(8,128)(2,1)S(1)}, bf16[128,256]{0,1:T(8,128)(2,1)S(1)}, u32[]{:S(2)}, u32[]{:S(2)}) collective-permute-start(bf16[128,256]{0,1:T(8,128)(2,1)S(1)} %copy.443), channel_id=1, source_target_pairs={{0,4},{1,5},{2,6},{3,7},{4,0},{5,1},{6,2},{7,3},{8,12},{9,13},{10,... | collective-permute-start | bytes 196616 | tf_op jit(solution)/shard_map/ppermute | solution.py:29
  8.6 45.5 %collective-permute-start.4 = (bf16[128,256]{0,1:T(8,128)(2,1)S(1)}, bf16[128,256]{0,1:T(8,128)(2,1)S(1)}, u32[]{:S(2)}, u32[]{:S(2)}) collective-permute-start(bf16[128,256]{0,1:T(8,128)(2,1)S(1)} %copy.444), channel_id=1, source_target_pairs={{0,5},{1,4},{2,7},{3,6},{4,1},{5,0},{6,3},{7,2},{8,13},{9,12},{10,... | collective-permute-start | bytes 196616 | tf_op jit(solution)/shard_map/ppermute | solution.py:29
  8.7 10.4 all-to-all-start.1
  16.0 17.4 %copy-start.6 = (bf16[128,2048]{1,0:T(8,128)(2,1)S(1)}, bf16[128,2048]{1,0:T(8,128)(2,1)}, u32[]{:S(2)}) copy-start(bf16[128,2048]{1,0:T(8,128)(2,1)} %param.18) | copy-start | bytes 1572868
  19.1 13.1 %copy-start.28 = (bf16[128,8,2]{0,2,1:T(2,128)(2,1)}, bf16[128,8,2]{0,2,1:T(2,128)(2,1)S(1)}, u32[]{:S(2)}) copy-start(bf16[128,8,2]{0,2,1:T(2,128)(2,1)S(1)} %all-to-all-done.1) | copy-start | bytes 12292
  19.1 8.7 all-to-all-start
  27.8 22.1 %all-to-all-start.3 = ((bf16[128,8,256]{0,2,1:T(8,128)(2,1)}), bf16[128,8,256]{0,2,1:T(8,128)(2,1)S(1)}, u32[]{:S(2)}, u32[]{:S(2)}) async-start(bf16[128,8,256]{0,2,1:T(8,128)(2,1)} %bitcast.20), calls=%async_computation.3 | async-start | bytes 1048576 | tf_op jit(solution)/shard_map/all_to_all | solution.py:173
  34.4 19.8 %copy-start.25 = (f32[1,2,8,128]{3,2,1,0:T(8,128)}, f32[1,2,8,128]{3,2,1,0:T(8,128)S(1)}, u32[]{:S(2)}) copy-start(f32[1,2,8,128]{3,2,1,0:T(8,128)S(1)} %divide_bitcast_fusion) | copy-start | bytes 24580
  35.6 18.5 %collective-permute-start.5 = (bf16[128,256]{0,1:T(8,128)(2,1)S(1)}, bf16[128,256]{0,1:T(8,128)(2,1)S(1)}, u32[]{:S(2)}, u32[]{:S(2)}) collective-permute-start(bf16[128,256]{0,1:T(8,128)(2,1)S(1)} %copy.445), channel_id=1, source_target_pairs={{0,6},{1,7},{2,4},{3,5},{4,2},{5,3},{6,0},{7,1},{8,14},{9,15},{10,... | collective-permute-start | bytes 196616 | tf_op jit(solution)/shard_map/ppermute | solution.py:29
  39.4 14.7 %collective-permute-start.6 = (bf16[128,256]{0,1:T(8,128)(2,1)S(1)}, bf16[128,256]{0,1:T(8,128)(2,1)S(1)}, u32[]{:S(2)}, u32[]{:S(2)}) collective-permute-start(bf16[128,256]{0,1:T(8,128)(2,1)S(1)} %copy.446), channel_id=1, source_target_pairs={{0,7},{1,6},{2,5},{3,4},{4,3},{5,2},{6,1},{7,0},{8,15},{9,14},{10,... | collective-permute-start | bytes 196616 | tf_op jit(solution)/shard_map/ppermute | solution.py:29
  49.9 19.5 %all-to-all-start.2 = ((bf16[128,8,256]{0,2,1:T(8,128)(2,1)}), bf16[128,8,256]{0,2,1:T(8,128)(2,1)}, u32[]{:S(2)}, u32[]{:S(2)}) async-start(bf16[128,8,256]{0,2,1:T(8,128)(2,1)} %bitcast.15), calls=%async_computation.2 | async-start | bytes 1048576 | tf_op jit(solution)/shard_map/all_to_all | solution.py:175
  69.4 21.1 %all-to-all-start.4 = ((bf16[128,8,256]{0,2,1:T(8,128)(2,1)}), bf16[128,8,256]{0,2,1:T(8,128)(2,1)}, u32[]{:S(2)}, u32[]{:S(2)}) async-start(bf16[128,8,256]{0,2,1:T(8,128)(2,1)} %bitcast.627), calls=%async_computation.4 | async-start | bytes 1048576 | tf_op jit(solution)/shard_map/all_to_all | solution.py:176
  103.5 27.1 %copy-start.1 = (f32[2,128]{1,0:T(2,128)}, f32[2,128]{1,0:T(2,128)S(1)}, u32[]{:S(2)}) copy-start(f32[2,128]{1,0:T(2,128)S(1)} %reduce_window_sum.46) | copy-start | bytes 3076 | tf_op jit(solution)/shard_map/jvp()/while
  109.4 30.3 %copy-start.7 = (f32[2,128]{1,0:T(2,128)S(1)}, f32[2,128]{1,0:T(2,128)}, u32[]{:S(2)}) copy-start(f32[2,128]{1,0:T(2,128)} %get-tuple-element.3083) | copy-start | bytes 3076 | tf_op jit(solution)/shard_map/jvp()/while
  146.0 27.2 %copy-start.1 = (f32[2,128]{1,0:T(2,128)}, f32[2,128]{1,0:T(2,128)S(1)}, u32[]{:S(2)}) copy-start(f32[2,128]{1,0:T(2,128)S(1)} %reduce_window_sum.46) | copy-start | bytes 3076 | tf_op jit(solution)/shard_map/jvp()/while
  151.9 31.2 %copy-start.7 = (f32[2,128]{1,0:T(2,128)S(1)}, f32[2,128]{1,0:T(2,128)}, u32[]{:S(2)}) copy-start(f32[2,128]{1,0:T(2,128)} %get-tuple-element.3083) | copy-start | bytes 3076 | tf_op jit(solution)/shard_map/jvp()/while
  173.2 10.7 %copy-start.9 = (f32[2,128]{1,0:T(2,128)S(1)}, f32[2,128]{1,0:T(2,128)}, u32[]{:S(2)}) copy-start(f32[2,128]{1,0:T(2,128)} %get-tuple-element.3084) | copy-start | bytes 3076 | tf_op jit(solution)/shard_map/jvp()/while
  176.4 10.0 copy-start.2
  189.5 27.2 %copy-start.1 = (f32[2,128]{1,0:T(2,128)}, f32[2,128]{1,0:T(2,128)S(1)}, u32[]{:S(2)}) copy-start(f32[2,128]{1,0:T(2,128)S(1)} %reduce_window_sum.46) | copy-start | bytes 3076 | tf_op jit(solution)/shard_map/jvp()/while
  195.4 31.2 %copy-start.7 = (f32[2,128]{1,0:T(2,128)S(1)}, f32[2,128]{1,0:T(2,128)}, u32[]{:S(2)}) copy-start(f32[2,128]{1,0:T(2,128)} %get-tuple-element.3083) | copy-start | bytes 3076 | tf_op jit(solution)/shard_map/jvp()/while
  216.6 10.7 %copy-start.9 = (f32[2,128]{1,0:T(2,128)S(1)}, f32[2,128]{1,0:T(2,128)}, u32[]{:S(2)}) copy-start(f32[2,128]{1,0:T(2,128)} %get-tuple-element.3084) | copy-start | bytes 3076 | tf_op jit(solution)/shard_map/jvp()/while
  232.9 27.2 %copy-start.1 = (f32[2,128]{1,0:T(2,128)}, f32[2,128]{1,0:T(2,128)S(1)}, u32[]{:S(2)}) copy-start(f32[2,128]{1,0:T(2,128)S(1)} %reduce_window_sum.46) | copy-start | bytes 3076 | tf_op jit(solution)/shard_map/jvp()/while
  238.8 31.2 %copy-start.7 = (f32[2,128]{1,0:T(2,128)S(1)}, f32[2,128]{1,0:T(2,128)}, u32[]{:S(2)}) copy-start(f32[2,128]{1,0:T(2,128)} %get-tuple-element.3083) | copy-start | bytes 3076 | tf_op jit(solution)/shard_map/jvp()/while
  260.1 10.7 %copy-start.9 = (f32[2,128]{1,0:T(2,128)S(1)}, f32[2,128]{1,0:T(2,128)}, u32[]{:S(2)}) copy-start(f32[2,128]{1,0:T(2,128)} %get-tuple-element.3084) | copy-start | bytes 3076 | tf_op jit(solution)/shard_map/jvp()/while
  276.3 27.1 %copy-start.1 = (f32[2,128]{1,0:T(2,128)}, f32[2,128]{1,0:T(2,128)S(1)}, u32[]{:S(2)}) copy-start(f32[2,128]{1,0:T(2,128)S(1)} %reduce_window_sum.46) | copy-start | bytes 3076 | tf_op jit(solution)/shard_map/jvp()/while
  282.3 31.2 %copy-start.7 = (f32[2,128]{1,0:T(2,128)S(1)}, f32[2,128]{1,0:T(2,128)}, u32[]{:S(2)}) copy-start(f32[2,128]{1,0:T(2,128)} %get-tuple-element.3083) | copy-start | bytes 3076 | tf_op jit(solution)/shard_map/jvp()/while
  303.5 10.7 %copy-start.9 = (f32[2,128]{1,0:T(2,128)S(1)}, f32[2,128]{1,0:T(2,128)}, u32[]{:S(2)}) copy-start(f32[2,128]{1,0:T(2,128)} %get-tuple-element.3084) | copy-start | bytes 3076 | tf_op jit(solution)/shard_map/jvp()/while
  319.8 27.1 %copy-start.1 = (f32[2,128]{1,0:T(2,128)}, f32[2,128]{1,0:T(2,128)S(1)}, u32[]{:S(2)}) copy-start(f32[2,128]{1,0:T(2,128)S(1)} %reduce_window_sum.46) | copy-start | bytes 3076 | tf_op jit(solution)/shard_map/jvp()/while
  325.7 31.2 %copy-start.7 = (f32[2,128]{1,0:T(2,128)S(1)}, f32[2,128]{1,0:T(2,128)}, u32[]{:S(2)}) copy-start(f32[2,128]{1,0:T(2,128)} %get-tuple-element.3083) | copy-start | bytes 3076 | tf_op jit(solution)/shard_map/jvp()/while
  346.9 10.7 %copy-start.9 = (f32[2,128]{1,0:T(2,128)S(1)}, f32[2,128]{1,0:T(2,128)}, u32[]{:S(2)}) copy-start(f32[2,128]{1,0:T(2,128)} %get-tuple-element.3084) | copy-start | bytes 3076 | tf_op jit(solution)/shard_map/jvp()/while
  363.2 27.1 %copy-start.1 = (f32[2,128]{1,0:T(2,128)}, f32[2,128]{1,0:T(2,128)S(1)}, u32[]{:S(2)}) copy-start(f32[2,128]{1,0:T(2,128)S(1)} %reduce_window_sum.46) | copy-start | bytes 3076 | tf_op jit(solution)/shard_map/jvp()/while
  369.2 31.2 %copy-start.7 = (f32[2,128]{1,0:T(2,128)S(1)}, f32[2,128]{1,0:T(2,128)}, u32[]{:S(2)}) copy-start(f32[2,128]{1,0:T(2,128)} %get-tuple-element.3083) | copy-start | bytes 3076 | tf_op jit(solution)/shard_map/jvp()/while
  390.4 10.7 %copy-start.9 = (f32[2,128]{1,0:T(2,128)S(1)}, f32[2,128]{1,0:T(2,128)}, u32[]{:S(2)}) copy-start(f32[2,128]{1,0:T(2,128)} %get-tuple-element.3084) | copy-start | bytes 3076 | tf_op jit(solution)/shard_map/jvp()/while
  406.7 27.2 %copy-start.1 = (f32[2,128]{1,0:T(2,128)}, f32[2,128]{1,0:T(2,128)S(1)}, u32[]{:S(2)}) copy-start(f32[2,128]{1,0:T(2,128)S(1)} %reduce_window_sum.46) | copy-start | bytes 3076 | tf_op jit(solution)/shard_map/jvp()/while
  412.6 31.1 %copy-start.7 = (f32[2,128]{1,0:T(2,128)S(1)}, f32[2,128]{1,0:T(2,128)}, u32[]{:S(2)}) copy-start(f32[2,128]{1,0:T(2,128)} %get-tuple-element.3083) | copy-start | bytes 3076 | tf_op jit(solution)/shard_map/jvp()/while
  433.8 10.7 %copy-start.9 = (f32[2,128]{1,0:T(2,128)S(1)}, f32[2,128]{1,0:T(2,128)}, u32[]{:S(2)}) copy-start(f32[2,128]{1,0:T(2,128)} %get-tuple-element.3084) | copy-start | bytes 3076 | tf_op jit(solution)/shard_map/jvp()/while
  977.4 15.9 %copy-start.20 = (f32[2,1024]{1,0:T(2,128)S(1)}, f32[2,1024]{1,0:T(2,128)}, u32[]{:S(2)}) copy-start(f32[2,1024]{1,0:T(2,128)} %copy-done.19) | copy-start | bytes 24580
  979.8 10.3 all-to-all-start.8
  990.1 8.7 all-to-all-start.9
  998.8 18.8 %all-to-all-start.6 = ((bf16[8,128,256]{1,2,0:T(8,128)(2,1)}), bf16[8,128,256]{1,2,0:T(8,128)(2,1)S(1)}, u32[]{:S(2)}, u32[]{:S(2)}) async-start(bf16[8,128,256]{1,2,0:T(8,128)(2,1)} %copy.406), calls=%async_computation.6 | async-start | bytes 1048576 | tf_op jit(solution)/shard_map/all_to_all | solution.py:191
  1004.4 16.7 %copy-start.3 = (bf16[8,2,128,128]{3,2,0,1:T(8,128)(2,1)S(1)}, bf16[8,2,128,128]{3,2,0,1:T(8,128)(2,1)}, u32[]{:S(2)}) copy-start(bf16[8,2,128,128]{3,2,0,1:T(8,128)(2,1)} %get-tuple-element.1507) | copy-start | bytes 1572868
  1017.6 18.8 %all-to-all-start.5 = ((bf16[8,128,256]{1,2,0:T(8,128)(2,1)}), bf16[8,128,256]{1,2,0:T(8,128)(2,1)S(1)}, u32[]{:S(2)}, u32[]{:S(2)}) async-start(bf16[8,128,256]{1,2,0:T(8,128)(2,1)} %copy.402), calls=%async_computation.5 | async-start | bytes 1048576 | tf_op jit(solution)/shard_map/all_to_all | solution.py:190
  1036.4 18.8 %all-to-all-start.7 = ((bf16[8,128,256]{1,2,0:T(8,128)(2,1)}), bf16[8,128,256]{1,2,0:T(8,128)(2,1)S(1)}, u32[]{:S(2)}, u32[]{:S(2)}) async-start(bf16[8,128,256]{1,2,0:T(8,128)(2,1)} %copy.409), calls=%async_computation.7 | async-start | bytes 1048576 | tf_op jit(solution)/shard_map/all_to_all | solution.py:192
  (78 other events, 367.4 us)
